TPU v7x, 512 devices: a whole 4x4x16 slice. The times are simulated.
512 devices in a mesh: seq: 64 (over y, z), head: 8 (over x, core).
Axes of the slice: x: 4, y: 4, z: 16, core: 2. Of those that a mesh axis runs over, the one named last changes fastest.
Arguments:
- hidden_in: bfloat16 [16384, 4096], P('seq', 'head'), may hold values from -6 to 6
- proj_weight: bfloat16 [4096, 256], replicated, may hold values from -0.09375 to 0.09375
- head_input: bfloat16 [16384, 8192], P('seq', 'head'), may hold values from -6 to 6
- gate_input: bfloat16 [16384, 8192], P('seq', 'head'), may hold values from -11 to 11
- step_size: float32 [16384, 128], P('seq', 'head'), may hold values from 0 to 4, as said below
- decay_rate: float32 [128], P('head'), may hold values from 0 to 1, as said below
- norm_gain: float32 [8192], P('head'), may hold values from 0.1 to 1.9
Outputs:
- layer_out: bfloat16 [16384, 8192], P('seq', 'head')
Inputs may be any that keep to these rules, and one draw needn't show every extreme that they name: `decay_rate`: positive. `step_size`: positive.
All inputs are finite; a program needn't handle non-finite values.
Results may differ from a plain program's by a relative error of at most 0.013.
Values may be sent and summed in bfloat16 or wider, within the bound.
A program may use at most 128 MiB of HBM per device.

v0:
```python
import jax
import jax.numpy as jnp
from jax import lax
from jax.sharding import PartitionSpec as P

HEADS = 128
HEAD_DIM = 64
STATE = 128
GROUP = 256


def carried_in(value, axis, join, neutral):
    count, mine = (lax.axis_size(axis), lax.axis_index(axis))
    pieces = jax.tree.map(lambda part: lax.all_gather(part, axis), value)
    running = jax.tree.map(
        lambda part, zero: jnp.full_like(part, 0) + jnp.asarray(zero, part.dtype), value, neutral
    )

    def step(position, running):
        longer = join(running, jax.tree.map(lambda part: part[position], pieces))
        return jax.tree.map(lambda new, old: jnp.where(position < mine, new, old), longer, running)

    return lax.fori_loop(0, count - 1, step, running)


def combine_states(earlier, later):
    return (earlier[0] + later[0], jnp.exp(later[0])[:, None, None] * earlier[1] + later[1])


def shards(hidden_in, proj_weight, head_input, gate_input, step_size, decay_rate, norm_gain):
    tok_rows = hidden_in.shape[0]
    local_heads = step_size.shape[1]
    summed = jnp.dot(
        lax.all_gather(hidden_in, "head", axis=1, tiled=True),
        proj_weight,
        preferred_element_type=jnp.float32,
    )
    projected = summed.astype(jnp.bfloat16)
    count = tok_rows // GROUP
    b_rows = projected[:, :STATE].reshape(count, GROUP, STATE)
    c_rows = projected[:, STATE:].reshape(count, GROUP, STATE)
    log_decay = -step_size * decay_rate[None, :]
    cumulative = jnp.cumsum(log_decay.reshape(count, GROUP, local_heads), axis=1)
    scaled = (
        head_input.reshape(tok_rows, local_heads, HEAD_DIM).astype(jnp.float32)
        * step_size[:, :, None]
    ).astype(jnp.bfloat16)
    scaled = scaled.reshape(count, GROUP, local_heads, HEAD_DIM)
    positions = jnp.arange(GROUP, dtype=jnp.int32)
    causal = positions[:, None] >= positions[None, :]
    scores = jnp.einsum("ctn,csn->cts", c_rows, b_rows, preferred_element_type=jnp.float32)
    cum_heads = jnp.swapaxes(cumulative, 1, 2)
    gap = cum_heads[:, :, :, None] - cum_heads[:, :, None, :]
    weights = jnp.exp(jnp.where(causal[None, None], gap, -jnp.inf))
    mixing = (scores[:, None] * weights).astype(jnp.bfloat16)
    inner = jnp.einsum("chts,cshp->cthp", mixing, scaled, preferred_element_type=jnp.float32)
    ends = cumulative[:, -1, :]
    tail = jnp.exp(ends[:, None, :] - cumulative)
    weighted = (tail[:, :, :, None] * scaled.astype(jnp.float32)).astype(jnp.bfloat16)
    fresh = jnp.einsum("cshp,csn->chpn", weighted, b_rows, preferred_element_type=jnp.float32)
    block_state = jnp.zeros((local_heads, HEAD_DIM, STATE), jnp.float32)
    block_state = jnp.exp(ends[0])[:, None, None] * block_state + fresh[0]
    block_decay = jnp.sum(ends, axis=0)
    identity = (
        jnp.zeros((local_heads,), jnp.float32),
        jnp.zeros((local_heads, HEAD_DIM, STATE), jnp.float32),
    )
    decay_total, incoming = carried_in((block_decay, block_state), "seq", combine_states, identity)
    entering = [incoming]
    carried_low = jnp.stack(entering).astype(jnp.bfloat16)
    outer = jnp.einsum("ctn,chpn->cthp", c_rows, carried_low, preferred_element_type=jnp.float32)
    outer = outer * jnp.exp(cumulative)[:, :, :, None]
    mixed = (inner + outer).reshape(tok_rows, local_heads * HEAD_DIM)
    gated = mixed * jax.nn.silu(gate_input.astype(jnp.float32))
    squares = jnp.sum(gated * gated, axis=1)
    total_squares = lax.psum(squares, "head")
    mean_square = total_squares / (HEADS * HEAD_DIM)
    return (gated * lax.rsqrt(mean_square + 1e-05)[:, None] * norm_gain[None, :]).astype(
        jnp.bfloat16
    )


def solution(mesh):
    in_specs = (
        P("seq", "head"),
        P(),
        P("seq", "head"),
        P("seq", "head"),
        P("seq", "head"),
        P("head"),
        P("head"),
    )
    out_specs = P("seq", "head")
    return jax.shard_map(shards, mesh=mesh, in_specs=in_specs, out_specs=out_specs, check_vma=False)
```

profile of v0, /device:TPU:1, one launch (start us, length us, event | category | flops | bytes accessed | tf_op | source)
XLA Modules:
  0.0 524.2 jit_solution(10919568476322371059)
XLA Ops:
  9.5 1.2 copy.29
  11.6 36.5 %all-gather.5.cloned.1.call-done = bf16[256,4096]{1,0:T(8,128)(2,1)} async-done(((bf16[256,512]{1,0:T(8,128)(2,1)}), bf16[256,4096]{1,0:T(8,128)(2,1)}) %all-gather.5.cloned.1.call-update) | async-done | bytes 2097168 | tf_op jit(solution)/shard_map/all_gather | solution.py:34
  48.1 2.3 convolution_convert_fusion
  52.3 70.7 %all-gather = f32[64,1,16]{2,1,0:T(1,128)} all-gather(f32[1,1,16]{2,1,0:T(1,128)S(1)} %copy.34), channel_id=2, replica_groups=mesh['seq'=64,'head'=8] {'seq'}, dimensions={0}, use_global_device_ids=true | all-gather | bytes 4160 | tf_op jit(solution)/shard_map/all_gather | solution.py:14
  124.5 219.6 %all-gather.7.cloned.1.call-done = f32[1024,64,128]{2,1,0:T(8,128)} async-done(((f32[16,64,128]{2,1,0:T(8,128)}), f32[1024,64,128]{2,1,0:T(8,128)}) %all-gather.7.cloned.1.call-update) | async-done | bytes 33554448 | tf_op jit(solution)/shard_map/all_gather | solution.py:14
  344.1 150.7 %while.14 = (s32[]{:T(128)}, f32[16,64,128]{2,1,0:T(8,128)S(1)}, s32[]{:T(128)}, f32[64,16]{1,0:T(8,128)}, f32[64,16,64,128]{3,2,1,0:T(8,128)}, /*index=5*/s32[]{:T(128)}, s32[]{:T(128)}) while((s32[]{:T(128)}, f32[16,64,128]{2,1,0:T(8,128)S(1)}, s32[]{:T(128)}, f32[64,16]{1,0:T(8,128)}, f32[64,16,64,128]{3,2,1,0:T(8,128)}, ...), condition=%wide.region_3.4_spmd.clone, body=%wide.region_2.3_spmd.clone.sunk | while | flops 524292 | bytes 1573161 | solution.py:23
  344.1 1.2 exponential_bitcast_fusion.2
  346.5 1.2 exponential_bitcast_fusion.2
  348.9 1.2 exponential_bitcast_fusion.2
  351.3 1.2 exponential_bitcast_fusion.2
  353.7 1.2 exponential_bitcast_fusion.2
  358.5 1.2 exponential_bitcast_fusion.2
  363.2 1.2 exponential_bitcast_fusion.2
  365.6 1.2 exponential_bitcast_fusion.2
  368.0 1.2 exponential_bitcast_fusion.2
  370.4 1.2 exponential_bitcast_fusion.2
  372.8 1.2 exponential_bitcast_fusion.2
  375.2 1.2 exponential_bitcast_fusion.2
  377.6 1.2 exponential_bitcast_fusion.2
  380.0 1.2 exponential_bitcast_fusion.2
  478.0 1.2 exponential_bitcast_fusion.2
  480.4 1.2 exponential_bitcast_fusion.2
  482.8 1.2 exponential_bitcast_fusion.2
  485.2 1.2 exponential_bitcast_fusion.2
  487.6 1.2 exponential_bitcast_fusion.2
  490.0 1.2 exponential_bitcast_fusion.2
  492.4 1.2 exponential_bitcast_fusion.2
  495.8 3.1 fusion.9
  498.9 1.6 copy.37
  500.5 1.4 multiply_reduce_fusion
  501.9 13.2 %psum.7 = f32[256]{0:T(256)S(1)} all-reduce(f32[256]{0:T(256)S(1)} %multiply_reduce_fusion), channel_id=1, replica_groups=mesh['seq'=64,'head'=8] {'head'}, use_global_device_ids=true, to_apply=%region_5.6 | all-reduce | flops 256 | bytes 2048 | tf_op jit(solution)/shard_map/psum | solution.py:76
  515.1 2.2 multiply_convert_fusion.6
  (139 shorter events, 132.2 us)
Async XLA Ops:
  6.5 41.6 %copy-start = (bf16[4096,256]{1,0:T(8,128)(2,1)S(1)}, bf16[4096,256]{1,0:T(8,128)(2,1)}, u32[]{:S(2)}) copy-start(bf16[4096,256]{1,0:T(8,128)(2,1)} %param.10) | copy-start | bytes 6291460
  6.5 41.6 %all-gather.5.cloned.1.call-start = ((), (), s32[]{:S(2)}) async-start(), calls=%async_computation | async-start | bytes 2359296 | tf_op jit(solution)/shard_map/all_gather | solution.py:34
  7.3 336.8 %all-gather.7.cloned.1.call-start = ((), (), s32[]{:S(2)}) async-start(), calls=%async_computation.1 | async-start | bytes 34078720 | tf_op jit(solution)/shard_map/all_gather | solution.py:14
  344.1 151.7 %copy-start.1 = (f32[256,16]{0,1:T(8,128)S(1)}, f32[256,16]{0,1:T(8,128)}, u32[]{:S(2)}) copy-start(f32[256,16]{0,1:T(8,128)} %param.13) | copy-start | bytes 49156
  495.8 19.3 %copy-start.2 = (f32[1024]{0:T(1024)S(1)}, f32[1024]{0:T(1024)}, u32[]{:S(2)}) copy-start(f32[1024]{0:T(1024)} %param.15) | copy-start | bytes 12292
Sparse Core Ops, SparseCore 0:
  9.5 38.6 all-gather.4
  51.7 292.3 all-gather.6
where the time goes:
time: 528 us; the launch traced here: 524 us
  waiting for transfers between devices  257 us (49%)
  blocking collectives  83.9 us (16%)
  other arithmetic  81 us (15%)
  local copies, waits for them, and re-layouts  79.9 us (15%)
  between operations  13.5 us (3%)
  matrix products  7.67 us (1%)
    all_gather x1, waiting for transfers between devices, carried_in(): pieces = jax.tree.map(lambda part: lax.all_gather(part, axis), value)  220 us
    exp x63, local copies, waits for them, and re-layouts, combine_states(): jnp.exp(later[0])[:, None, None] * earlier[1] + later[1]  75.8 us
    select_n x63, other arithmetic, step(): jnp.where(position < mine, new, old)  73.7 us
    all_gather x1, blocking collectives, carried_in(): pieces = jax.tree.map(lambda part: lax.all_gather(part, axis), value)  70.7 us
    all_gather x1, waiting for transfers between devices, shards(): lax.all_gather(hidden_in, 'head', axis=1, tiled=True)  36.5 us
    psum x1, blocking collectives, shards(): total_squares = lax.psum(squares, 'head')  13.2 us
  transfers between devices with their start and end apart: 2, of which 2 were waited for; matrix products, arithmetic and copies ran while one was open for 1% of the time, Pallas kernels for 0%

commit v1 on v0

v1 whole, which is shorter than its diff:
```python
import functools
import math

import jax
import jax.numpy as jnp
from jax import lax
from jax.experimental import pallas as pl
from jax.experimental.pallas import tpu as pltpu
from jax.sharding import PartitionSpec as P

MESH = pl.DeviceIdType.MESH
F32, BF16 = jnp.float32, jnp.bfloat16
T = 256
HEADS = 16
HEAD_DIM = 64
STATE = 128
COLS = HEADS * HEAD_DIM
HALF = COLS // 2
LOG2E = math.log2(math.e)


def dot(a, b):
    return jnp.dot(a, b, preferred_element_type=F32)


def kernel(
    NH, NY, NZ,
    hid, w, x, g, dt, rate, gain, out,
    hid_v, w_v, x_v, g_v, dt_v, rate_v, gain_v, in_sem,
    part, rsr, agr, scl, wgt, expand,
    fsend, frecv, dsend, drecv, ysend, yrecv, gsend, grecv,
    acc, fac, gated_v, srecv,
    rs_s, rs_r, ag_s, ag_r, d_s, d_r, f_s, f_r, y_s, y_r, g_s, g_r, s_s, s_r,
):
    KD = hid_v.shape[1]
    RB = T // NH
    NI = NZ // 2
    me_h = lax.axis_index("head")
    seq = lax.axis_index("seq")
    me_z = lax.rem(seq, NZ)
    me_y = lax.div(seq, NZ)

    def head_peer(r):
        return lax.rem(me_h + r, NH)

    def z_peer(r):
        return lax.rem(me_z + r, NZ)

    def y_peer(r):
        return lax.rem(me_y + r, NY)

    def seq_id(y, z):
        return y * NZ + z

    barrier = pltpu.get_barrier_semaphore()

    @pl.loop(1, NH)
    def _(r):
        pl.semaphore_signal(barrier, inc=1, device_id={"head": head_peer(r)}, device_id_type=MESH)

    @pl.loop(1, NZ)
    def _(r):
        pl.semaphore_signal(barrier, inc=1, device_id={"seq": seq_id(me_y, z_peer(r))}, device_id_type=MESH)

    @pl.loop(1, NY)
    def _(r):
        pl.semaphore_signal(barrier, inc=1, device_id={"seq": seq_id(y_peer(r), me_z)}, device_id_type=MESH)

    loads = [
        pltpu.make_async_copy(hid, hid_v, in_sem.at[0]),
        pltpu.make_async_copy(w.at[pl.ds(pl.multiple_of(me_h * KD, KD), KD)], w_v, in_sem.at[1]),
        pltpu.make_async_copy(dt, dt_v, in_sem.at[2]),
        pltpu.make_async_copy(rate, rate_v, in_sem.at[3]),
        pltpu.make_async_copy(x, x_v, in_sem.at[4]),
        pltpu.make_async_copy(g, g_v, in_sem.at[5]),
        pltpu.make_async_copy(gain, gain_v, in_sem.at[6]),
    ]
    for load in loads:
        load.start()
    loads[0].wait()
    loads[1].wait()
    part[...] = dot(hid_v[...], w_v[...]).reshape(NH, RB, 2 * STATE)

    def rs_copy(src, dst_peer, slot):
        return pltpu.make_async_remote_copy(
            src_ref=part.at[src], dst_ref=rsr.at[slot], send_sem=rs_s.at[src], recv_sem=rs_r.at[slot],
            device_id={"head": dst_peer}, device_id_type=MESH)

    def ag_copy(peer, slot):
        return pltpu.make_async_remote_copy(
            src_ref=agr.at[slot], dst_ref=agr.at[slot], send_sem=ag_s.at[peer], recv_sem=ag_r.at[slot],
            device_id={"head": peer}, device_id_type=MESH)

    def d_copy(peer, slot):
        return pltpu.make_async_remote_copy(
            src_ref=dsend.at[lax.div(peer, NI)], dst_ref=drecv.at[slot], send_sem=d_s.at[peer], recv_sem=d_r.at[slot],
            device_id={"seq": seq_id(me_y, peer)}, device_id_type=MESH)

    def f_copy(peer, slot):
        return pltpu.make_async_remote_copy(
            src_ref=fsend.at[peer], dst_ref=frecv.at[slot], send_sem=f_s.at[peer], recv_sem=f_r.at[slot],
            device_id={"seq": seq_id(me_y, peer)}, device_id_type=MESH)

    def y_copy(peer, slot):
        return pltpu.make_async_remote_copy(
            src_ref=ysend, dst_ref=yrecv.at[slot], send_sem=y_s.at[peer], recv_sem=y_r.at[slot],
            device_id={"seq": seq_id(peer, me_z)}, device_id_type=MESH)

    def g_copy(peer, slot):
        return pltpu.make_async_remote_copy(
            src_ref=gsend.at[peer], dst_ref=grecv.at[slot], send_sem=g_s.at[peer], recv_sem=g_r.at[slot],
            device_id={"seq": seq_id(me_y, peer)}, device_id_type=MESH)

    def s_copy(peer, slot):
        return pltpu.make_async_remote_copy(
            src_ref=srecv.at[slot], dst_ref=srecv.at[slot], send_sem=s_s.at[peer], recv_sem=s_r.at[slot],
            device_id={"head": peer}, device_id_type=MESH)

    def each(n, peer_of, action):
        @pl.loop(1, n)
        def _(r):
            action(peer_of(r))

    pl.semaphore_wait(barrier, (NH - 1) + (NZ - 1) + (NY - 1))
    each(NH, head_peer, lambda p: rs_copy(p, p, me_h).start())

    loads[2].wait()
    loads[3].wait()
    lane = lax.broadcasted_iota(jnp.int32, (T, 128), 1)
    low_lane = lane < HEAD_DIM
    rows = lax.broadcasted_iota(jnp.int32, (T, T), 0)
    cols = lax.broadcasted_iota(jnp.int32, (T, T), 1)
    causal = rows >= cols
    tri = jnp.where(causal, 1.0, 0.0).astype(BF16)
    log_decay = -(dt_v[...] * rate_v[...])
    log_decay = jnp.concatenate([log_decay, jnp.zeros((T, 128 - HEADS), F32)], axis=1)
    top = log_decay.astype(BF16)
    rest = log_decay - top.astype(F32)
    mid = rest.astype(BF16)
    low = (rest - mid.astype(F32)).astype(BF16)
    cum = ((dot(tri, low) + dot(tri, mid)) + dot(tri, top)) * LOG2E
    cum_end = cum[T - 1:T, :]
    grow = jnp.exp2(cum)
    tail = jnp.exp2(cum_end - cum)

    def spread(value, q, n):
        a = jnp.broadcast_to(value[:, 2 * q:2 * q + 1], (n, 128))
        b = jnp.broadcast_to(value[:, 2 * q + 1:2 * q + 2], (n, 128))
        return jnp.where(low_lane[:n], a, b)

    for q in range(HEADS // 2):
        at = pl.ds(128 * q, 128)
        e = spread(grow, q, T)
        expand[:, at] = e
        dsend[q // (HEADS // 4), :, pl.ds(128 * (q % (HEADS // 4)), 128)] = e[T - 1:T, :]
    each(NZ, z_peer, lambda p: d_copy(p, me_z).start())
    drecv[pl.ds(me_z, 1)] = dsend[pl.ds(lax.div(me_z, NI), 1)]

    loads[4].wait()
    dt_all = dt_v[...]
    for q in range(HEADS // 2):
        at = pl.ds(128 * q, 128)
        s = (x_v[:, at].astype(F32) * spread(dt_all, q, T)).astype(BF16)
        scl[:, at] = s
        wgt[:, at] = (spread(tail, q, T) * s.astype(F32)).astype(BF16)

    total = part[pl.ds(me_h, 1)]
    each(NH, head_peer, lambda p: rs_copy(p, p, p).wait_recv())
    rsr[pl.ds(me_h, 1)] = total
    total = rsr[0]
    for k in range(1, NH):
        total = total + rsr[k]
    agr[pl.ds(me_h, 1)] = total.astype(BF16)[None]
    each(NH, head_peer, lambda p: ag_copy(p, me_h).start())
    each(NH, head_peer, lambda p: ag_copy(p, p).wait_recv())
    projected = agr[...].reshape(T, 2 * STATE)
    b_rows = projected[:, :STATE]
    c_rows = projected[:, STATE:]
    b_cols = b_rows.astype(F32).T.astype(BF16)

    SR = STATE // NI
    for j in range(2):
        fresh = dot(b_cols, wgt[:, pl.ds(HALF * j, HALF)]).astype(BF16)
        fsend[pl.ds(NI * j, NI)] = fresh.reshape(NI, SR, HALF)
    each(NZ, z_peer, lambda p: f_copy(p, me_z).start())
    frecv[pl.ds(me_z, 1)] = fsend[pl.ds(me_z, 1)]

    loads[5].wait()
    scores = dot(c_rows, b_cols)
    M = T // 2
    tri_half = causal[:M, :M]
    s00 = jnp.where(tri_half, scores[:M, :M], 0.0)
    s10 = scores[M:, :M]
    s11 = jnp.where(tri_half, scores[M:, M:], 0.0)
    cum_rows = cum.T
    low_half = low_lane[:T]
    for q in range(HEADS // 2):
        at = pl.ds(128 * q, 128)
        mix = []
        for h in (2 * q, 2 * q + 1):
            down = jnp.broadcast_to(cum[:, h:h + 1], (T, M))
            along = cum_rows[h:h + 1, :]
            m00 = s00 * jnp.exp2(jnp.minimum(down[:M] - along[:, :M], 0.0))
            m10 = s10 * jnp.exp2(down[M:] - along[:, :M])
            m11 = s11 * jnp.exp2(jnp.minimum(down[M:] - along[:, M:], 0.0))
            mix.append((m00.astype(BF16), jnp.concatenate([m10.astype(BF16), m11.astype(BF16)], axis=1)))
        s = scl[:, at]
        zero = jnp.zeros_like(s)
        sa = jnp.where(low_half, s, zero)
        sb = jnp.where(low_half, zero, s)
        upper = dot(jnp.concatenate([mix[0][0], mix[1][0]], axis=1), jnp.concatenate([sa[:M], sb[:M]], axis=0))
        lower = dot(mix[0][1], sa) + dot(mix[1][1], sb)
        v = g_v[:, at].astype(F32)
        silu = v / (1.0 + jnp.exp(-v))
        fac[:, at] = expand[:, at] * silu
        acc[:M, at] = upper * silu[:M]
        acc[M:, at] = lower * silu[M:]

    each(NZ, z_peer, lambda p: d_copy(p, p).wait_recv())
    each(NZ, z_peer, lambda p: f_copy(p, p).wait_recv())
    carry = frecv[0].astype(F32)
    span = drecv[0]
    for k in range(1, NZ):
        carry = drecv[k] * carry + frecv[k].astype(F32)
        span = drecv[k] * span
    ysend[:SR] = carry
    ysend[SR:] = jnp.broadcast_to(span, (8, HALF))
    each(NY, y_peer, lambda p: y_copy(p, me_y).start())
    yrecv[pl.ds(me_y, 1)] = ysend[...][None]
    each(NY, y_peer, lambda p: y_copy(p, p).wait_recv())
    carry = jnp.zeros((SR, HALF), F32)
    for k in range(NY - 1):
        later = yrecv[k, SR:SR + 1] * carry + yrecv[k, :SR]
        carry = jnp.where(k < me_y, later, carry)
    for k in range(NZ):
        gsend[k] = carry.astype(BF16)
        carry = drecv[k] * carry + frecv[k].astype(F32)
    each(NZ, z_peer, lambda p: g_copy(p, me_z).start())
    grecv[pl.ds(me_z, 1)] = gsend[pl.ds(me_z, 1)]
    each(NZ, z_peer, lambda p: g_copy(p, p).wait_recv())

    squares = jnp.zeros((T, 128), F32)
    for j in range(2):
        entering = grecv[pl.ds(NI * j, NI)].reshape(STATE, HALF)
        at = pl.ds(HALF * j, HALF)
        gated = acc[:, at] + dot(c_rows, entering) * fac[:, at]
        gated_v[:, at] = gated
        sq = gated * gated
        for i in range(HALF // 128):
            squares = squares + sq[:, 128 * i:128 * i + 128]
    srecv[pl.ds(me_h, 1)] = jnp.sum(squares.T, axis=0, keepdims=True)[None]
    each(NH, head_peer, lambda p: s_copy(p, me_h).start())
    each(NH, head_peer, lambda p: s_copy(p, p).wait_recv())
    mean = srecv[0]
    for k in range(1, NH):
        mean = mean + srecv[k]
    mean = mean / (NH * COLS)
    scale = lax.rsqrt(jnp.broadcast_to(mean, (128, T)) + 1e-05).T
    loads[6].wait()
    for q in range(HEADS // 2):
        at = pl.ds(128 * q, 128)
        out[:, at] = (gated_v[:, at] * scale * gain_v[:, at]).astype(BF16)

    each(NH, head_peer, lambda p: rs_copy(p, p, me_h).wait_send())
    each(NH, head_peer, lambda p: ag_copy(p, me_h).wait_send())
    each(NH, head_peer, lambda p: s_copy(p, me_h).wait_send())
    each(NZ, z_peer, lambda p: d_copy(p, me_z).wait_send())
    each(NZ, z_peer, lambda p: f_copy(p, me_z).wait_send())
    each(NZ, z_peer, lambda p: g_copy(p, me_z).wait_send())
    each(NY, y_peer, lambda p: y_copy(p, me_y).wait_send())


def shards(NH, NY, NZ, hidden_in, proj_weight, head_input, gate_input, step_size, decay_rate, norm_gain):
    KD = hidden_in.shape[1]
    RB = T // NH
    SR = STATE // (NZ // 2)
    any_space = pl.BlockSpec(memory_space=pl.ANY)
    vm, dma = pltpu.VMEM, pltpu.SemaphoreType.DMA
    return pl.pallas_call(
        functools.partial(kernel, NH, NY, NZ),
        name="layer",
        out_shape=jax.ShapeDtypeStruct((T, COLS), BF16),
        in_specs=[any_space] * 7,
        out_specs=pl.BlockSpec(memory_space=pltpu.VMEM),
        scratch_shapes=[
            vm((T, KD), BF16), vm((KD, 2 * STATE), BF16), vm((T, COLS), BF16), vm((T, COLS), BF16),
            vm((T, HEADS), F32), vm((1, HEADS), F32), vm((1, COLS), F32), dma((7,)),
            vm((NH, RB, 2 * STATE), F32), vm((NH, RB, 2 * STATE), F32), vm((NH, RB, 2 * STATE), BF16),
            vm((T, COLS), BF16), vm((T, COLS), BF16), vm((T, COLS), F32),
            vm((NZ, SR, HALF), BF16), vm((NZ, SR, HALF), BF16), vm((2, 1, HALF), F32), vm((NZ, 1, HALF), F32),
            vm((SR + 8, HALF), F32), vm((NY, SR + 8, HALF), F32), vm((NZ, SR, HALF), BF16), vm((NZ, SR, HALF), BF16),
            vm((T, COLS), F32), vm((T, COLS), F32), vm((T, COLS), F32), vm((NH, 1, T), F32),
            dma((NH,)), dma((NH,)), dma((NH,)), dma((NH,)), dma((NZ,)), dma((NZ,)), dma((NZ,)), dma((NZ,)),
            dma((NY,)), dma((NY,)), dma((NZ,)), dma((NZ,)), dma((NH,)), dma((NH,)),
        ],
        compiler_params=pltpu.CompilerParams(collective_id=0, has_side_effects=True),
    )(hidden_in, proj_weight, head_input, gate_input, step_size, decay_rate.reshape(1, HEADS), norm_gain.reshape(1, COLS))


def solution(mesh):
    NZ = 16
    NY = mesh.shape["seq"] // NZ
    NH = mesh.shape["head"]
    in_specs = (
        P("seq", "head"), P(), P("seq", "head"), P("seq", "head"), P("seq", "head"), P("head"), P("head"),
    )
    return jax.shard_map(
        functools.partial(shards, NH, NY, NZ), mesh=mesh, in_specs=in_specs, out_specs=P("seq", "head"), check_vma=False)
```

time: 528 us -> 69.4 us (0.13)
  waiting for transfers between devices: 257 us -> 0 us
  blocking collectives: 83.9 us -> 0 us
  other arithmetic: 81 us -> 0 us
  local copies, waits for them, and re-layouts: 79.9 us -> 3.34 us
  Pallas kernels: 0 us -> 65.8 us
  between operations: 13.5 us -> 0.01 us
  matrix products: 7.67 us -> 0 us
    all_gather x2 -> x0, waiting for transfers between devices: 256 us -> none  [the longest x1 220 us: carried_in(): pieces = jax.tree.map(lambda part: lax.all_gather(part, axis), value)]
    exp x63 -> x0, local copies, waits for them, and re-layouts: 75.8 us -> none  [combine_states(): jnp.exp(later[0])[:, None, None] * earlier[1] + later[1]]
    select_n x63 -> x0, other arithmetic: 73.7 us -> none  [step(): jnp.where(position < mine, new, old)]
    all_gather x1 -> x0, blocking collectives: 70.7 us -> none  [carried_in(): pieces = jax.tree.map(lambda part: lax.all_gather(part, axis), value)]
    pallas_call x0 -> x1, Pallas kernels: none -> 65.8 us  [shards(): pl.pallas_call(functools.partial(kernel, NH, NY, NZ), name='layer', out_s...]
    psum x1 -> x0, blocking collectives: 13.2 us -> none  [shards(): total_squares = lax.psum(squares, 'head')]
    dot_general x5 -> x0, matrix products: 7.67 us -> none  [the longest x1 3.1 us: shards(): jnp.einsum('chts,cshp->cthp', mixing, scaled, preferred_element_type=jnp....]
  transfers between devices with their start and end apart: 2 -> 0, of which waited for: 2 -> 0; matrix products, arithmetic and copies ran while one was open for 1% -> 0% of each run, Pallas kernels for 0% -> 0%
where the time goes in v1:
time: 69.4 us; the launch traced here: 69.1 us
  Pallas kernels  65.8 us (95%)
  local copies, waits for them, and re-layouts  3.34 us (5%)
    pallas_call x1, Pallas kernels, shards(): pl.pallas_call(functools.partial(kernel, NH, NY, NZ), name='layer', out_s...  65.8 us
    unnamed x2, local copies, waits for them, and re-layouts  3.34 us

profile of v1, /device:TPU:1, one launch (start us, length us, event | category | flops | bytes accessed | tf_op | source)
XLA Modules:
  0.0 69.1 jit_solution(7676080398705016496)
XLA Ops:
  0.0 1.5 %copy.8.dt = f32[256,16]{1,0:T(8,128)} copy(f32[256,16]{0,1:T(8,128)} %param.11) | data formatting | bytes 32768 | tf_op args[4]
  1.5 65.8 %layer.1 = bf16[256,1024]{1,0:T(8,128)(2,1)} custom-call(bf16[256,512]{1,0:T(8,128)(2,1)} %hid.1, bf16[4096,256]{1,0:T(8,128)(2,1)} %w.1, bf16[256,1024]{1,0:T(8,128)(2,1)} %x.1, bf16[256,1024]{1,0:T(8,128)(2,1)} %g.1, f32[256,16]{1,0:T(8,128)} %copy.8.dt, f32[1,16]{1,0:T(1,128)} %bitcast.3, f32[1,1024]{1,0:T(1,128)} %bitcast.2), custom_call_target="tpu_custom_call" | custom-call | tf_op jit(solution)/shard_map/layer/pallas_call | solution.py:279
  67.3 1.9 %copy.10 = bf16[256,1024]{1,0:T(8,128)(2,1)} copy(bf16[256,1024]{1,0:T(8,128)(2,1)} %layer.1) | data formatting | bytes 1048576

commit v2 on v1

v2 whole, which is shorter than its diff:
```python
import functools
import math

import jax
import jax.numpy as jnp
from jax import lax
from jax.experimental import pallas as pl
from jax.experimental.pallas import tpu as pltpu
from jax.sharding import PartitionSpec as P

MESH = pl.DeviceIdType.MESH
F32, BF16 = jnp.float32, jnp.bfloat16
T = 256
HEADS = 16
HEAD_DIM = 64
STATE = 128
COLS = HEADS * HEAD_DIM
HALF = COLS // 2
CW = HALF // 2
LOG2E = math.log2(math.e)


def dot(a, b):
    return jnp.dot(a, b, preferred_element_type=F32)


def kernel(
    NH, NY, NZ,
    hid, w, x, g, dt, rate, gain, out,
    hid_v, w_v, x_v, g_v, dt_v, rate_v, gain_v, in_sem,
    part, rsr, agr, scl, wgt, expand,
    fsend, frecv, dsend, drecv, ysend, yrecv, gsend, grecv,
    acc, fac, gated_v, srecv,
    rs_s, rs_r, ag_s, ag_r, d_s, d_r, f_s, f_r, y_s, y_r, g_s, g_r, s_s, s_r, from_left, from_right,
):
    KD = hid_v.shape[1]
    RB = T // NH
    NI = NZ // 2
    SR = STATE // NI
    me_h = lax.axis_index("head")
    seq = lax.axis_index("seq")
    me_z = lax.rem(seq, NZ)
    me_y = lax.div(seq, NZ)

    def head_peer(r):
        return lax.rem(me_h + r, NH)

    def far_first(k):
        off = lax.div(k, 2)
        return NZ // 2 + jnp.where(lax.rem(k, 2) == 1, off, -off)

    def z_peer(k):
        return lax.rem(me_z + far_first(k), NZ)

    def y_peer(r):
        return lax.rem(me_y + r, NY)

    def seq_id(y, z):
        return y * NZ + z

    right = {"seq": seq_id(me_y, lax.rem(me_z + 1, NZ))}
    left = {"seq": seq_id(me_y, lax.rem(me_z + NZ - 1, NZ))}

    def each(n, peer_of, action):
        @pl.loop(1, n)
        def _(r):
            action(peer_of(r))

    def signal(sem, device):
        pl.semaphore_signal(sem, inc=1, device_id=device, device_id_type=MESH)

    barrier = pltpu.get_barrier_semaphore()
    signal(barrier, right)
    signal(barrier, left)
    each(NH, head_peer, lambda p: signal(barrier, {"head": p}))
    each(NY, y_peer, lambda p: signal(barrier, {"seq": seq_id(p, me_z)}))

    loads = [
        pltpu.make_async_copy(hid, hid_v, in_sem.at[0]),
        pltpu.make_async_copy(w.at[pl.ds(pl.multiple_of(me_h * KD, KD), KD)], w_v, in_sem.at[1]),
        pltpu.make_async_copy(dt, dt_v, in_sem.at[2]),
        pltpu.make_async_copy(rate, rate_v, in_sem.at[3]),
        pltpu.make_async_copy(x, x_v, in_sem.at[4]),
        pltpu.make_async_copy(g, g_v, in_sem.at[5]),
        pltpu.make_async_copy(gain, gain_v, in_sem.at[6]),
    ]
    for load in loads:
        load.start()
    loads[0].wait()
    loads[1].wait()
    own = dot(hid_v[...], w_v[...])
    for m in range(2):
        part[m] = own[:, STATE * m:STATE * m + STATE].reshape(NH, RB, STATE)

    def remote(src, dst, send_sem, recv_sem, device):
        return pltpu.make_async_remote_copy(
            src_ref=src, dst_ref=dst, send_sem=send_sem, recv_sem=recv_sem, device_id=device, device_id_type=MESH)

    def rs_copy(m, peer, slot):
        return remote(part.at[m, peer], rsr.at[m, slot], rs_s.at[m, peer], rs_r.at[m, slot], {"head": peer})

    def ag_copy(m, peer, slot):
        return remote(agr.at[m, slot], agr.at[m, slot], ag_s.at[m, peer], ag_r.at[m, slot], {"head": peer})

    def d_copy(peer, slot):
        return remote(dsend.at[lax.div(peer, NI)], drecv.at[slot], d_s.at[peer], d_r.at[slot], {"seq": seq_id(me_y, peer)})

    def f_copy(c, peer, slot):
        return remote(fsend.at[c, peer], frecv.at[c, slot], f_s.at[c, peer], f_r.at[c, slot], {"seq": seq_id(me_y, peer)})

    def y_copy(c, peer, slot):
        return remote(ysend.at[c], yrecv.at[c, slot], y_s.at[c, peer], y_r.at[c, slot], {"seq": seq_id(peer, me_z)})

    def g_copy(c, peer, slot):
        return remote(gsend.at[c, peer], grecv.at[c, slot], g_s.at[c, peer], g_r.at[c, slot], {"seq": seq_id(me_y, peer)})

    def s_copy(peer, slot):
        return remote(srecv.at[slot], srecv.at[slot], s_s.at[peer], s_r.at[slot], {"head": peer})

    pl.semaphore_wait(barrier, (NH - 1) + (NY - 1) + 2)
    for m in range(2):
        each(NH, head_peer, lambda p: rs_copy(m, p, me_h).start())

    def relay():
        signal(from_left, right)
        signal(from_right, left)
        pl.semaphore_wait(from_left, 1)
        pl.semaphore_wait(from_right, 1)

    loads[2].wait()
    loads[3].wait()
    lane = lax.broadcasted_iota(jnp.int32, (T, 128), 1)
    low_lane = lane < HEAD_DIM
    rows = lax.broadcasted_iota(jnp.int32, (T, T), 0)
    cols = lax.broadcasted_iota(jnp.int32, (T, T), 1)
    causal = rows >= cols
    tri = jnp.where(causal, 1.0, 0.0).astype(BF16)
    dt_all = jnp.concatenate([dt_v[...], jnp.zeros((128 - HEADS, T), F32)], axis=0).T
    rate_all = jnp.concatenate([rate_v[...], jnp.zeros((1, 128 - HEADS), F32)], axis=1)
    log_decay = -(dt_all * rate_all)
    top = log_decay.astype(BF16)
    rest = log_decay - top.astype(F32)
    mid = rest.astype(BF16)
    low = (rest - mid.astype(F32)).astype(BF16)
    cum = ((dot(tri, low) + dot(tri, mid)) + dot(tri, top)) * LOG2E
    cum_end = cum[T - 1:T, :]
    grow = jnp.exp2(cum)
    tail = jnp.exp2(cum_end - cum)

    def spread(value, q):
        a = jnp.broadcast_to(value[:, 2 * q:2 * q + 1], (T, 128))
        b = jnp.broadcast_to(value[:, 2 * q + 1:2 * q + 2], (T, 128))
        return jnp.where(low_lane, a, b)

    hops = NZ // 2 - 1
    for q in range(HEADS // 2):
        if q < hops:
            relay()
        at = pl.ds(128 * q, 128)
        e = spread(grow, q)
        expand[:, at] = e
        dsend[(q % 4) // 2, q // 4, :, pl.ds(128 * (q % 2), 128)] = e[T - 1:T, :]

    loads[4].wait()
    for q in range(HEADS // 2):
        at = pl.ds(128 * q, 128)
        s = (x_v[:, at].astype(F32) * spread(dt_all, q)).astype(BF16)
        scl[:, at] = s
        wgt[:, at] = (spread(tail, q) * s.astype(F32)).astype(BF16)
    each(NZ, z_peer, lambda p: d_copy(p, me_z).start())
    drecv[pl.ds(me_z, 1)] = dsend[pl.ds(lax.div(me_z, NI), 1)]

    for m in range(2):
        rsr[m, pl.ds(me_h, 1)] = part[m, pl.ds(me_h, 1)]
        each(NH, head_peer, lambda p: rs_copy(m, p, p).wait_recv())
        total = rsr[m, 0]
        for k in range(1, NH):
            total = total + rsr[m, k]
        agr[m, pl.ds(me_h, 1)] = total.astype(BF16)[None]
        each(NH, head_peer, lambda p: ag_copy(m, p, me_h).start())
    each(NH, head_peer, lambda p: ag_copy(0, p, p).wait_recv())
    b_cols = agr[0].reshape(T, STATE).astype(F32).T.astype(BF16)

    for c in range(2):
        for j in range(2):
            fresh = dot(b_cols, wgt[:, pl.ds(HALF * c + CW * j, CW)]).astype(BF16)
            fsend[c, pl.ds(NI * j, NI)] = fresh.reshape(NI, SR, CW)
        each(NZ, z_peer, lambda p: f_copy(c, p, me_z).start())
        frecv[c, pl.ds(me_z, 1)] = fsend[c, pl.ds(me_z, 1)]

    each(NH, head_peer, lambda p: ag_copy(1, p, p).wait_recv())
    c_rows = agr[1].reshape(T, STATE)
    loads[5].wait()
    scores = dot(c_rows, b_cols)
    M = T // 2
    tri_half = causal[:M, :M]
    s00 = jnp.where(tri_half, scores[:M, :M], 0.0)
    s10 = scores[M:, :M]
    s11 = jnp.where(tri_half, scores[M:, M:], 0.0)
    cum_rows = cum.T
    for q in range(HEADS // 2):
        at = pl.ds(128 * q, 128)
        mix = []
        for h in (2 * q, 2 * q + 1):
            down = jnp.broadcast_to(cum[:, h:h + 1], (T, M))
            along = cum_rows[h:h + 1, :]
            m00 = s00 * jnp.exp2(jnp.minimum(down[:M] - along[:, :M], 0.0))
            m10 = s10 * jnp.exp2(down[M:] - along[:, :M])
            m11 = s11 * jnp.exp2(jnp.minimum(down[M:] - along[:, M:], 0.0))
            mix.append((m00.astype(BF16), jnp.concatenate([m10.astype(BF16), m11.astype(BF16)], axis=1)))
        s = scl[:, at]
        zero = jnp.zeros_like(s)
        sa = jnp.where(low_lane, s, zero)
        sb = jnp.where(low_lane, zero, s)
        upper = dot(jnp.concatenate([mix[0][0], mix[1][0]], axis=1), jnp.concatenate([sa[:M], sb[:M]], axis=0))
        lower = dot(mix[0][1], sa) + dot(mix[1][1], sb)
        v = g_v[:, at].astype(F32)
        silu = v / (1.0 + jnp.exp(-v))
        fac[:, at] = expand[:, at] * silu
        acc[:M, at] = upper * silu[:M]
        acc[M:, at] = lower * silu[M:]

    each(NZ, z_peer, lambda p: d_copy(p, p).wait_recv())
    for c in range(2):
        each(NZ, z_peer, lambda p: f_copy(c, p, p).wait_recv())
        carry = frecv[c, 0].astype(F32)
        span = drecv[0, c]
        for k in range(1, NZ):
            carry = drecv[k, c] * carry + frecv[c, k].astype(F32)
            span = drecv[k, c] * span
        ysend[c, :SR] = carry
        ysend[c, SR:] = jnp.broadcast_to(span, (8, CW))
        each(NY, y_peer, lambda p: y_copy(c, p, me_y).start())
        yrecv[c, pl.ds(me_y, 1)] = ysend[c][None]
    for c in range(2):
        each(NY, y_peer, lambda p: y_copy(c, p, p).wait_recv())
        carry = jnp.zeros((SR, CW), F32)
        for k in range(NY - 1):
            later = yrecv[c, k, SR:SR + 1] * carry + yrecv[c, k, :SR]
            carry = jnp.where(k < me_y, later, carry)
        for k in range(NZ):
            gsend[c, k] = carry.astype(BF16)
            carry = drecv[k, c] * carry + frecv[c, k].astype(F32)
        each(NZ, z_peer, lambda p: g_copy(c, p, me_z).start())
        grecv[c, pl.ds(me_z, 1)] = gsend[c, pl.ds(me_z, 1)]

    squares = jnp.zeros((T, 128), F32)
    for c in range(2):
        each(NZ, z_peer, lambda p: g_copy(c, p, p).wait_recv())
        for j in range(2):
            entering = grecv[c, pl.ds(NI * j, NI)].reshape(STATE, CW)
            at = pl.ds(HALF * c + CW * j, CW)
            gated = acc[:, at] + dot(c_rows, entering) * fac[:, at]
            gated_v[:, at] = gated
            sq = gated * gated
            for i in range(CW // 128):
                squares = squares + sq[:, 128 * i:128 * i + 128]
    srecv[pl.ds(me_h, 1)] = jnp.sum(squares.T, axis=0, keepdims=True)[None]
    each(NH, head_peer, lambda p: s_copy(p, me_h).start())
    each(NH, head_peer, lambda p: s_copy(p, p).wait_recv())
    mean = srecv[0]
    for k in range(1, NH):
        mean = mean + srecv[k]
    mean = mean / (NH * COLS)
    scale = lax.rsqrt(jnp.broadcast_to(mean, (128, T)) + 1e-05).T
    loads[6].wait()
    for q in range(HEADS // 2):
        at = pl.ds(128 * q, 128)
        out[:, at] = (gated_v[:, at] * scale * gain_v[:, at]).astype(BF16)

    for m in range(2):
        each(NH, head_peer, lambda p: rs_copy(m, p, me_h).wait_send())
        each(NH, head_peer, lambda p: ag_copy(m, p, me_h).wait_send())
    each(NH, head_peer, lambda p: s_copy(p, me_h).wait_send())
    each(NZ, z_peer, lambda p: d_copy(p, me_z).wait_send())
    for c in range(2):
        each(NZ, z_peer, lambda p: f_copy(c, p, me_z).wait_send())
        each(NZ, z_peer, lambda p: g_copy(c, p, me_z).wait_send())
        each(NY, y_peer, lambda p: y_copy(c, p, me_y).wait_send())


def shards(NH, NY, NZ, hidden_in, proj_weight, head_input, gate_input, step_size, decay_rate, norm_gain):
    KD = hidden_in.shape[1]
    RB = T // NH
    SR = STATE // (NZ // 2)
    operands = (hidden_in, proj_weight, head_input, gate_input, step_size.T, decay_rate.reshape(1, HEADS), norm_gain.reshape(1, COLS))
    in_hbm = pl.BlockSpec(memory_space=pltpu.HBM)
    vm, dma = pltpu.VMEM, pltpu.SemaphoreType.DMA
    return pl.pallas_call(
        functools.partial(kernel, NH, NY, NZ),
        name="layer",
        out_shape=jax.ShapeDtypeStruct((T, COLS), BF16),
        in_specs=[in_hbm] * 7,
        out_specs=pl.BlockSpec(memory_space=pltpu.VMEM),
        scratch_shapes=[
            vm((T, KD), BF16), vm((KD, 2 * STATE), BF16), vm((T, COLS), BF16), vm((T, COLS), BF16),
            vm((HEADS, T), F32), vm((1, HEADS), F32), vm((1, COLS), F32), dma((7,)),
            vm((2, NH, RB, STATE), F32), vm((2, NH, RB, STATE), F32), vm((2, NH, RB, STATE), BF16),
            vm((T, COLS), BF16), vm((T, COLS), BF16), vm((T, COLS), F32),
            vm((2, NZ, SR, CW), BF16), vm((2, NZ, SR, CW), BF16), vm((2, 2, 1, CW), F32), vm((NZ, 2, 1, CW), F32),
            vm((2, SR + 8, CW), F32), vm((2, NY, SR + 8, CW), F32), vm((2, NZ, SR, CW), BF16), vm((2, NZ, SR, CW), BF16),
            vm((T, COLS), F32), vm((T, COLS), F32), vm((T, COLS), F32), vm((NH, 1, T), F32),
            dma((2, NH)), dma((2, NH)), dma((2, NH)), dma((2, NH)), dma((NZ,)), dma((NZ,)), dma((2, NZ)), dma((2, NZ)),
            dma((2, NY)), dma((2, NY)), dma((2, NZ)), dma((2, NZ)), dma((NH,)), dma((NH,)),
            pltpu.SemaphoreType.REGULAR, pltpu.SemaphoreType.REGULAR,
        ],
        compiler_params=pltpu.CompilerParams(collective_id=0, has_side_effects=True, vmem_limit_bytes=20 * 2**20),
    )(*(pltpu.with_memory_space_constraint(operand, pltpu.HBM) for operand in operands))


def solution(mesh):
    NZ = 16
    NY = mesh.shape["seq"] // NZ
    NH = mesh.shape["head"]
    in_specs = (
        P("seq", "head"), P(), P("seq", "head"), P("seq", "head"), P("seq", "head"), P("head"), P("head"),
    )
    return jax.shard_map(
        functools.partial(shards, NH, NY, NZ), mesh=mesh, in_specs=in_specs, out_specs=P("seq", "head"), check_vma=False)
```

time: 69.4 us -> 70 us (level)
  Pallas kernels: 65.8 us -> 69.1 us
  local copies, waits for them, and re-layouts: 3.34 us -> 0.8 us
    pallas_call x1, Pallas kernels: 65.8 us -> 69.1 us  [shards(): pl.pallas_call(functools.partial(kernel, NH, NY, NZ), name='layer', out_s...]
    unnamed x2 -> x1, local copies, waits for them, and re-layouts: 3.34 us -> 0.8 us
where the time goes in v2:
time: 70 us; the launch traced here: 69.9 us
  Pallas kernels  69.1 us (99%)
  local copies, waits for them, and re-layouts  0.8 us (1%)
    pallas_call x1, Pallas kernels, shards(): pl.pallas_call(functools.partial(kernel, NH, NY, NZ), name='layer', out_s...  69.1 us

profile of v2, /device:TPU:1, one launch (start us, length us, event | category | flops | bytes accessed | tf_op | source)
XLA Modules:
  0.0 69.9 jit_solution(15762494955048527621)
XLA Ops:
  0.0 69.1 %layer.1 = bf16[256,1024]{1,0:T(8,128)(2,1)S(1)} custom-call(bf16[256,512]{1,0:T(8,128)(2,1)} %hid.1, bf16[4096,256]{1,0:T(8,128)(2,1)} %w.1, bf16[256,1024]{1,0:T(8,128)(2,1)} %x.1, bf16[256,1024]{1,0:T(8,128)(2,1)} %g.1, f32[16,256]{1,0:T(8,128)} %bitcast.3, f32[1,16]{1,0:T(1,128)} %bitcast.5, f32[1,1024]{1,0:T(1,128)} %bitcast.4), custom_call_target="tpu_custom_call" | custom-call | tf_op jit(solution)/shard_map/layer/pallas_call | solution.py:289
  69.1 0.8 %copy.9 = bf16[256,1024]{1,0:T(8,128)(2,1)} copy(bf16[256,1024]{1,0:T(8,128)(2,1)S(1)} %layer.1) | data formatting | bytes 1048576

commit v3 on v2

--- a/solution.py
+++ b/solution.py
@@ -31,7 +31,7 @@
     part, rsr, agr, scl, wgt, expand,
     fsend, frecv, dsend, drecv, ysend, yrecv, gsend, grecv,
     acc, fac, gated_v, srecv,
-    rs_s, rs_r, ag_s, ag_r, d_s, d_r, f_s, f_r, y_s, y_r, g_s, g_r, s_s, s_r, from_left, from_right,
+    rs_s, rs_r, ag_s, ag_r, d_s, d_r, f_s, f_r, y_s, y_r, g_s, g_r, s_s, s_r,
 ):
     KD = hid_v.shape[1]
     RB = T // NH
@@ -58,9 +58,6 @@
     def seq_id(y, z):
         return y * NZ + z
 
-    right = {"seq": seq_id(me_y, lax.rem(me_z + 1, NZ))}
-    left = {"seq": seq_id(me_y, lax.rem(me_z + NZ - 1, NZ))}
-
     def each(n, peer_of, action):
         @pl.loop(1, n)
         def _(r):
@@ -70,10 +67,9 @@
         pl.semaphore_signal(sem, inc=1, device_id=device, device_id_type=MESH)
 
     barrier = pltpu.get_barrier_semaphore()
-    signal(barrier, right)
-    signal(barrier, left)
+    each(NZ, z_peer, lambda p: signal(barrier, {"seq": seq_id(me_y, p)}))
+    each(NY, y_peer, lambda p: signal(barrier, {"seq": seq_id(p, me_z)}))
     each(NH, head_peer, lambda p: signal(barrier, {"head": p}))
-    each(NY, y_peer, lambda p: signal(barrier, {"seq": seq_id(p, me_z)}))
 
     loads = [
         pltpu.make_async_copy(hid, hid_v, in_sem.at[0]),
@@ -117,15 +113,9 @@
     def s_copy(peer, slot):
         return remote(srecv.at[slot], srecv.at[slot], s_s.at[peer], s_r.at[slot], {"head": peer})
 
-    pl.semaphore_wait(barrier, (NH - 1) + (NY - 1) + 2)
+    pl.semaphore_wait(barrier, (NH - 1) + (NY - 1) + (NZ - 1))
     for m in range(2):
         each(NH, head_peer, lambda p: rs_copy(m, p, me_h).start())
-
-    def relay():
-        signal(from_left, right)
-        signal(from_right, left)
-        pl.semaphore_wait(from_left, 1)
-        pl.semaphore_wait(from_right, 1)
 
     loads[2].wait()
     loads[3].wait()
@@ -152,10 +142,7 @@
         b = jnp.broadcast_to(value[:, 2 * q + 1:2 * q + 2], (T, 128))
         return jnp.where(low_lane, a, b)
 
-    hops = NZ // 2 - 1
     for q in range(HEADS // 2):
-        if q < hops:
-            relay()
         at = pl.ds(128 * q, 128)
         e = spread(grow, q)
         expand[:, at] = e
@@ -302,7 +289,6 @@
             vm((T, COLS), F32), vm((T, COLS), F32), vm((T, COLS), F32), vm((NH, 1, T), F32),
             dma((2, NH)), dma((2, NH)), dma((2, NH)), dma((2, NH)), dma((NZ,)), dma((NZ,)), dma((2, NZ)), dma((2, NZ)),
             dma((2, NY)), dma((2, NY)), dma((2, NZ)), dma((2, NZ)), dma((NH,)), dma((NH,)),
-            pltpu.SemaphoreType.REGULAR, pltpu.SemaphoreType.REGULAR,
         ],
         compiler_params=pltpu.CompilerParams(collective_id=0, has_side_effects=True, vmem_limit_bytes=20 * 2**20),
     )(*(pltpu.with_memory_space_constraint(operand, pltpu.HBM) for operand in operands))

time: 70 us -> 62 us (0.89)
  Pallas kernels: 69.1 us -> 61.1 us
    pallas_call x1, Pallas kernels: 69.1 us -> 61.1 us  [shards(): pl.pallas_call(functools.partial(kernel, NH, NY, NZ), name='layer', out_s...]
where the time goes in v3:
time: 62 us; the launch traced here: 61.9 us
  Pallas kernels  61.1 us (99%)
  local copies, waits for them, and re-layouts  0.8 us (1%)
    pallas_call x1, Pallas kernels, shards(): pl.pallas_call(functools.partial(kernel, NH, NY, NZ), name='layer', out_s...  61.1 us

profile of v3, /device:TPU:1, one launch (start us, length us, event | category | flops | bytes accessed | tf_op | source)
XLA Modules:
  0.0 61.9 jit_solution(5598215478669873269)
XLA Ops:
  0.0 61.1 %layer.1 = bf16[256,1024]{1,0:T(8,128)(2,1)S(1)} custom-call(bf16[256,512]{1,0:T(8,128)(2,1)} %hid.1, bf16[4096,256]{1,0:T(8,128)(2,1)} %w.1, bf16[256,1024]{1,0:T(8,128)(2,1)} %x.1, bf16[256,1024]{1,0:T(8,128)(2,1)} %g.1, f32[16,256]{1,0:T(8,128)} %bitcast.3, f32[1,16]{1,0:T(1,128)} %bitcast.5, f32[1,1024]{1,0:T(1,128)} %bitcast.4), custom_call_target="tpu_custom_call" | custom-call | tf_op jit(solution)/shard_map/layer/pallas_call | solution.py:276
  61.1 0.8 %copy.9 = bf16[256,1024]{1,0:T(8,128)(2,1)} copy(bf16[256,1024]{1,0:T(8,128)(2,1)S(1)} %layer.1) | data formatting | bytes 1048576

commit v4 on v3

--- a/solution.py
+++ b/solution.py
@@ -15,8 +15,9 @@
 HEAD_DIM = 64
 STATE = 128
 COLS = HEADS * HEAD_DIM
-HALF = COLS // 2
-CW = HALF // 2
+CHUNKS = 2
+CHUNK = COLS // CHUNKS
+CW = CHUNK // 2
 LOG2E = math.log2(math.e)
 
 
@@ -31,7 +32,7 @@
     part, rsr, agr, scl, wgt, expand,
     fsend, frecv, dsend, drecv, ysend, yrecv, gsend, grecv,
     acc, fac, gated_v, srecv,
-    rs_s, rs_r, ag_s, ag_r, d_s, d_r, f_s, f_r, y_s, y_r, g_s, g_r, s_s, s_r,
+    rs_s, rs_r, ag_s, ag_r, d_s, d_r, f_s, f_r, y_s, y_r, g_s, g_r, s_s, s_r, token,
 ):
     KD = hid_v.shape[1]
     RB = T // NH
@@ -67,7 +68,15 @@
         pl.semaphore_signal(sem, inc=1, device_id=device, device_id_type=MESH)
 
     barrier = pltpu.get_barrier_semaphore()
-    each(NZ, z_peer, lambda p: signal(barrier, {"seq": seq_id(me_y, p)}))
+    def greet(sem, distance):
+        for step in (distance, NZ - distance):
+            signal(sem, {"seq": seq_id(me_y, lax.rem(me_z + step, NZ))})
+
+    greet(barrier, 1)
+    greet(barrier, 2)
+    strides = []
+    while 2 * 2 ** len(strides) < NZ // 2:
+        strides.append(2 * 2 ** len(strides))
     each(NY, y_peer, lambda p: signal(barrier, {"seq": seq_id(p, me_z)}))
     each(NH, head_peer, lambda p: signal(barrier, {"head": p}))
 
@@ -92,28 +101,32 @@
         return pltpu.make_async_remote_copy(
             src_ref=src, dst_ref=dst, send_sem=send_sem, recv_sem=recv_sem, device_id=device, device_id_type=MESH)
 
+    def drain(ref, sem):
+        pltpu.make_async_copy(ref, ref, sem).wait()
+
     def rs_copy(m, peer, slot):
-        return remote(part.at[m, peer], rsr.at[m, slot], rs_s.at[m, peer], rs_r.at[m, slot], {"head": peer})
+        return remote(part.at[m, peer], rsr.at[m, slot], rs_s, rs_r.at[m], {"head": peer})
 
     def ag_copy(m, peer, slot):
-        return remote(agr.at[m, slot], agr.at[m, slot], ag_s.at[m, peer], ag_r.at[m, slot], {"head": peer})
+        return remote(agr.at[m, slot], agr.at[m, slot], ag_s, ag_r.at[m], {"head": peer})
 
     def d_copy(peer, slot):
-        return remote(dsend.at[lax.div(peer, NI)], drecv.at[slot], d_s.at[peer], d_r.at[slot], {"seq": seq_id(me_y, peer)})
+        return remote(dsend.at[lax.div(peer, NI)], drecv.at[slot], d_s, d_r, {"seq": seq_id(me_y, peer)})
 
     def f_copy(c, peer, slot):
-        return remote(fsend.at[c, peer], frecv.at[c, slot], f_s.at[c, peer], f_r.at[c, slot], {"seq": seq_id(me_y, peer)})
+        return remote(fsend.at[c, peer], frecv.at[c, slot], f_s, f_r.at[c], {"seq": seq_id(me_y, peer)})
 
     def y_copy(c, peer, slot):
-        return remote(ysend.at[c], yrecv.at[c, slot], y_s.at[c, peer], y_r.at[c, slot], {"seq": seq_id(peer, me_z)})
+        return remote(ysend.at[c], yrecv.at[c, slot], y_s, y_r.at[c], {"seq": seq_id(peer, me_z)})
 
     def g_copy(c, peer, slot):
-        return remote(gsend.at[c, peer], grecv.at[c, slot], g_s.at[c, peer], g_r.at[c, slot], {"seq": seq_id(me_y, peer)})
+        return remote(gsend.at[c, peer], grecv.at[c, slot], g_s, g_r.at[c], {"seq": seq_id(me_y, peer)})
 
     def s_copy(peer, slot):
-        return remote(srecv.at[slot], srecv.at[slot], s_s.at[peer], s_r.at[slot], {"head": peer})
-
-    pl.semaphore_wait(barrier, (NH - 1) + (NY - 1) + (NZ - 1))
+        return remote(srecv.at[slot], srecv.at[slot], s_s, s_r, {"head": peer})
+
+    pl.semaphore_wait(barrier, (NH - 1) + (NY - 1) + 4)
+    greet(token.at[0], strides[0])
     for m in range(2):
         each(NH, head_peer, lambda p: rs_copy(m, p, me_h).start())
 
@@ -147,6 +160,9 @@
         e = spread(grow, q)
         expand[:, at] = e
         dsend[(q % 4) // 2, q // 4, :, pl.ds(128 * (q % 2), 128)] = e[T - 1:T, :]
+    for i, stride in enumerate(strides[1:]):
+        pl.semaphore_wait(token.at[i], 2)
+        greet(token.at[i + 1], stride)
 
     loads[4].wait()
     for q in range(HEADS // 2):
@@ -154,28 +170,30 @@
         s = (x_v[:, at].astype(F32) * spread(dt_all, q)).astype(BF16)
         scl[:, at] = s
         wgt[:, at] = (spread(tail, q) * s.astype(F32)).astype(BF16)
-    each(NZ, z_peer, lambda p: d_copy(p, me_z).start())
-    drecv[pl.ds(me_z, 1)] = dsend[pl.ds(lax.div(me_z, NI), 1)]
 
     for m in range(2):
         rsr[m, pl.ds(me_h, 1)] = part[m, pl.ds(me_h, 1)]
-        each(NH, head_peer, lambda p: rs_copy(m, p, p).wait_recv())
+        drain(rsr.at[m, pl.ds(0, NH - 1)], rs_r.at[m])
         total = rsr[m, 0]
         for k in range(1, NH):
             total = total + rsr[m, k]
         agr[m, pl.ds(me_h, 1)] = total.astype(BF16)[None]
         each(NH, head_peer, lambda p: ag_copy(m, p, me_h).start())
-    each(NH, head_peer, lambda p: ag_copy(0, p, p).wait_recv())
+    pl.semaphore_wait(token.at[len(strides) - 1], 2)
+    each(NZ, z_peer, lambda p: d_copy(p, me_z).start())
+    drecv[pl.ds(me_z, 1)] = dsend[pl.ds(lax.div(me_z, NI), 1)]
+    drain(agr.at[0, pl.ds(0, NH - 1)], ag_r.at[0])
     b_cols = agr[0].reshape(T, STATE).astype(F32).T.astype(BF16)
 
-    for c in range(2):
+
+    for c in range(CHUNKS):
+        fresh = dot(b_cols, wgt[:, pl.ds(CHUNK * c, CHUNK)]).astype(BF16)
         for j in range(2):
-            fresh = dot(b_cols, wgt[:, pl.ds(HALF * c + CW * j, CW)]).astype(BF16)
-            fsend[c, pl.ds(NI * j, NI)] = fresh.reshape(NI, SR, CW)
+            fsend[c, pl.ds(NI * j, NI)] = fresh[:, CW * j:CW * j + CW].reshape(NI, SR, CW)
         each(NZ, z_peer, lambda p: f_copy(c, p, me_z).start())
         frecv[c, pl.ds(me_z, 1)] = fsend[c, pl.ds(me_z, 1)]
 
-    each(NH, head_peer, lambda p: ag_copy(1, p, p).wait_recv())
+    drain(agr.at[1, pl.ds(0, NH - 1)], ag_r.at[1])
     c_rows = agr[1].reshape(T, STATE)
     loads[5].wait()
     scores = dot(c_rows, b_cols)
@@ -207,9 +225,9 @@
         acc[:M, at] = upper * silu[:M]
         acc[M:, at] = lower * silu[M:]
 
-    each(NZ, z_peer, lambda p: d_copy(p, p).wait_recv())
-    for c in range(2):
-        each(NZ, z_peer, lambda p: f_copy(c, p, p).wait_recv())
+    drain(drecv.at[pl.ds(0, NZ - 1)], d_r)
+    for c in range(CHUNKS):
+        drain(frecv.at[c, pl.ds(0, NZ - 1)], f_r.at[c])
         carry = frecv[c, 0].astype(F32)
         span = drecv[0, c]
         for k in range(1, NZ):
@@ -219,8 +237,9 @@
         ysend[c, SR:] = jnp.broadcast_to(span, (8, CW))
         each(NY, y_peer, lambda p: y_copy(c, p, me_y).start())
         yrecv[c, pl.ds(me_y, 1)] = ysend[c][None]
-    for c in range(2):
-        each(NY, y_peer, lambda p: y_copy(c, p, p).wait_recv())
+    for c in range(CHUNKS):
+        if NY > 1:
+            drain(yrecv.at[c, pl.ds(0, NY - 1)], y_r.at[c])
         carry = jnp.zeros((SR, CW), F32)
         for k in range(NY - 1):
             later = yrecv[c, k, SR:SR + 1] * carry + yrecv[c, k, :SR]
@@ -231,39 +250,38 @@
         each(NZ, z_peer, lambda p: g_copy(c, p, me_z).start())
         grecv[c, pl.ds(me_z, 1)] = gsend[c, pl.ds(me_z, 1)]
 
+    loads[6].wait()
     squares = jnp.zeros((T, 128), F32)
-    for c in range(2):
-        each(NZ, z_peer, lambda p: g_copy(c, p, p).wait_recv())
+    for c in range(CHUNKS):
+        drain(grecv.at[c, pl.ds(0, NZ - 1)], g_r.at[c])
         for j in range(2):
             entering = grecv[c, pl.ds(NI * j, NI)].reshape(STATE, CW)
-            at = pl.ds(HALF * c + CW * j, CW)
+            at = pl.ds(CHUNK * c + CW * j, CW)
             gated = acc[:, at] + dot(c_rows, entering) * fac[:, at]
-            gated_v[:, at] = gated
+            gated_v[:, at] = gated * gain_v[:, at]
             sq = gated * gated
             for i in range(CW // 128):
                 squares = squares + sq[:, 128 * i:128 * i + 128]
     srecv[pl.ds(me_h, 1)] = jnp.sum(squares.T, axis=0, keepdims=True)[None]
     each(NH, head_peer, lambda p: s_copy(p, me_h).start())
-    each(NH, head_peer, lambda p: s_copy(p, p).wait_recv())
+    drain(srecv.at[pl.ds(0, NH - 1)], s_r)
     mean = srecv[0]
     for k in range(1, NH):
         mean = mean + srecv[k]
     mean = mean / (NH * COLS)
     scale = lax.rsqrt(jnp.broadcast_to(mean, (128, T)) + 1e-05).T
-    loads[6].wait()
     for q in range(HEADS // 2):
         at = pl.ds(128 * q, 128)
-        out[:, at] = (gated_v[:, at] * scale * gain_v[:, at]).astype(BF16)
-
-    for m in range(2):
-        each(NH, head_peer, lambda p: rs_copy(m, p, me_h).wait_send())
-        each(NH, head_peer, lambda p: ag_copy(m, p, me_h).wait_send())
-    each(NH, head_peer, lambda p: s_copy(p, me_h).wait_send())
-    each(NZ, z_peer, lambda p: d_copy(p, me_z).wait_send())
-    for c in range(2):
-        each(NZ, z_peer, lambda p: f_copy(c, p, me_z).wait_send())
-        each(NZ, z_peer, lambda p: g_copy(c, p, me_z).wait_send())
-        each(NY, y_peer, lambda p: y_copy(c, p, me_y).wait_send())
+        out[:, at] = (gated_v[:, at] * scale).astype(BF16)
+
+    drain(part.at[:, pl.ds(0, NH - 1)], rs_s)
+    drain(agr.at[:, pl.ds(0, NH - 1)], ag_s)
+    drain(drecv.at[pl.ds(0, NZ - 1)], d_s)
+    drain(fsend.at[:, pl.ds(0, NZ - 1)], f_s)
+    drain(gsend.at[:, pl.ds(0, NZ - 1)], g_s)
+    drain(srecv.at[pl.ds(0, NH - 1)], s_s)
+    if NY > 1:
+        drain(yrecv.at[:, pl.ds(0, NY - 1)], y_s)
 
 
 def shards(NH, NY, NZ, hidden_in, proj_weight, head_input, gate_input, step_size, decay_rate, norm_gain):
@@ -284,11 +302,12 @@
             vm((HEADS, T), F32), vm((1, HEADS), F32), vm((1, COLS), F32), dma((7,)),
             vm((2, NH, RB, STATE), F32), vm((2, NH, RB, STATE), F32), vm((2, NH, RB, STATE), BF16),
             vm((T, COLS), BF16), vm((T, COLS), BF16), vm((T, COLS), F32),
-            vm((2, NZ, SR, CW), BF16), vm((2, NZ, SR, CW), BF16), vm((2, 2, 1, CW), F32), vm((NZ, 2, 1, CW), F32),
-            vm((2, SR + 8, CW), F32), vm((2, NY, SR + 8, CW), F32), vm((2, NZ, SR, CW), BF16), vm((2, NZ, SR, CW), BF16),
+            vm((CHUNKS, NZ, SR, CW), BF16), vm((CHUNKS, NZ, SR, CW), BF16), vm((2, CHUNKS, 1, CW), F32), vm((NZ, CHUNKS, 1, CW), F32),
+            vm((CHUNKS, SR + 8, CW), F32), vm((CHUNKS, NY, SR + 8, CW), F32),
+            vm((CHUNKS, NZ, SR, CW), BF16), vm((CHUNKS, NZ, SR, CW), BF16),
             vm((T, COLS), F32), vm((T, COLS), F32), vm((T, COLS), F32), vm((NH, 1, T), F32),
-            dma((2, NH)), dma((2, NH)), dma((2, NH)), dma((2, NH)), dma((NZ,)), dma((NZ,)), dma((2, NZ)), dma((2, NZ)),
-            dma((2, NY)), dma((2, NY)), dma((2, NZ)), dma((2, NZ)), dma((NH,)), dma((NH,)),
+            dma, dma((2,)), dma, dma((2,)), dma, dma, dma, dma((CHUNKS,)), dma, dma((CHUNKS,)), dma, dma((CHUNKS,)), dma, dma,
+            pltpu.SemaphoreType.REGULAR((2,)),
         ],
         compiler_params=pltpu.CompilerParams(collective_id=0, has_side_effects=True, vmem_limit_bytes=20 * 2**20),
     )(*(pltpu.with_memory_space_constraint(operand, pltpu.HBM) for operand in operands))

time: 62 us -> 56 us (0.903)
  Pallas kernels: 61.1 us -> 55.1 us
    pallas_call x1, Pallas kernels: 61.1 us -> 55.1 us  [shards(): pl.pallas_call(functools.partial(kernel, NH, NY, NZ), name='layer', out_s...]
where the time goes in v4:
time: 56 us; the launch traced here: 55.9 us
  Pallas kernels  55.1 us (98%)
  local copies, waits for them, and re-layouts  0.8 us (1%)
    pallas_call x1, Pallas kernels, shards(): pl.pallas_call(functools.partial(kernel, NH, NY, NZ), name='layer', out_s...  55.1 us

profile of v4, /device:TPU:1, one launch (start us, length us, event | category | flops | bytes accessed | tf_op | source)
XLA Modules:
  0.0 55.9 jit_solution(6401932535388912520)
XLA Ops:
  0.0 55.1 %layer.1 = bf16[256,1024]{1,0:T(8,128)(2,1)S(1)} custom-call(bf16[256,512]{1,0:T(8,128)(2,1)} %hid.1, bf16[4096,256]{1,0:T(8,128)(2,1)} %w.1, bf16[256,1024]{1,0:T(8,128)(2,1)} %x.1, bf16[256,1024]{1,0:T(8,128)(2,1)} %g.1, f32[16,256]{1,0:T(8,128)} %bitcast.3, f32[1,16]{1,0:T(1,128)} %bitcast.5, f32[1,1024]{1,0:T(1,128)} %bitcast.4), custom_call_target="tpu_custom_call" | custom-call | tf_op jit(solution)/shard_map/layer/pallas_call | solution.py:294
  55.1 0.8 %copy.9 = bf16[256,1024]{1,0:T(8,128)(2,1)} copy(bf16[256,1024]{1,0:T(8,128)(2,1)S(1)} %layer.1) | data formatting | bytes 1048576

commit v5 on v4

--- a/solution.py
+++ b/solution.py
@@ -29,16 +29,16 @@
     NH, NY, NZ,
     hid, w, x, g, dt, rate, gain, out,
     hid_v, w_v, x_v, g_v, dt_v, rate_v, gain_v, in_sem,
-    part, rsr, agr, scl, wgt, expand,
+    part, pair, agr, scl, wgt, expand,
     fsend, frecv, dsend, drecv, ysend, yrecv, gsend, grecv,
     acc, fac, gated_v, srecv,
-    rs_s, rs_r, ag_s, ag_r, d_s, d_r, f_s, f_r, y_s, y_r, g_s, g_r, s_s, s_r, token,
+    p_s, p_r, ag_s, ag_r, d_s, d_r, f_s, f_r, y_s, y_r, g_s, g_r, s_s, s_r, token,
 ):
     KD = hid_v.shape[1]
-    RB = T // NH
     NI = NZ // 2
     SR = STATE // NI
     me_h = lax.axis_index("head")
+    core = lax.rem(me_h, 2)
     seq = lax.axis_index("seq")
     me_z = lax.rem(seq, NZ)
     me_y = lax.div(seq, NZ)
@@ -64,21 +64,12 @@
         def _(r):
             action(peer_of(r))
 
+    def each_now(n, peer_of, action):
+        for r in range(1, n):
+            action(peer_of(r))
+
     def signal(sem, device):
         pl.semaphore_signal(sem, inc=1, device_id=device, device_id_type=MESH)
-
-    barrier = pltpu.get_barrier_semaphore()
-    def greet(sem, distance):
-        for step in (distance, NZ - distance):
-            signal(sem, {"seq": seq_id(me_y, lax.rem(me_z + step, NZ))})
-
-    greet(barrier, 1)
-    greet(barrier, 2)
-    strides = []
-    while 2 * 2 ** len(strides) < NZ // 2:
-        strides.append(2 * 2 ** len(strides))
-    each(NY, y_peer, lambda p: signal(barrier, {"seq": seq_id(p, me_z)}))
-    each(NH, head_peer, lambda p: signal(barrier, {"head": p}))
 
     loads = [
         pltpu.make_async_copy(hid, hid_v, in_sem.at[0]),
@@ -89,13 +80,29 @@
         pltpu.make_async_copy(g, g_v, in_sem.at[5]),
         pltpu.make_async_copy(gain, gain_v, in_sem.at[6]),
     ]
-    for load in loads:
+    loads[0].start()
+    loads[1].start()
+
+    barrier = pltpu.get_barrier_semaphore()
+    def greet(sem, distance):
+        for step in (distance, NZ - distance):
+            signal(sem, {"seq": seq_id(me_y, lax.rem(me_z + step, NZ))})
+
+    greet(barrier, 1)
+    greet(barrier, 2)
+    strides = []
+    while 2 * 2 ** len(strides) < NZ // 2:
+        strides.append(2 * 2 ** len(strides))
+    each_now(NY, y_peer, lambda p: signal(barrier, {"seq": seq_id(p, me_z)}))
+    each_now(NH, head_peer, lambda p: signal(barrier, {"head": p}))
+
+    for load in loads[2:]:
         load.start()
     loads[0].wait()
     loads[1].wait()
     own = dot(hid_v[...], w_v[...])
     for m in range(2):
-        part[m] = own[:, STATE * m:STATE * m + STATE].reshape(NH, RB, STATE)
+        part[m] = own[:, STATE * m:STATE * m + STATE].reshape(2, T // 2, STATE)
 
     def remote(src, dst, send_sem, recv_sem, device):
         return pltpu.make_async_remote_copy(
@@ -104,8 +111,8 @@
     def drain(ref, sem):
         pltpu.make_async_copy(ref, ref, sem).wait()
 
-    def rs_copy(m, peer, slot):
-        return remote(part.at[m, peer], rsr.at[m, slot], rs_s, rs_r.at[m], {"head": peer})
+    def pair_copy(m):
+        return remote(part.at[m, 1 - core], pair.at[m], p_s, p_r.at[m], {"head": me_h + 1 - 2 * core})
 
     def ag_copy(m, peer, slot):
         return remote(agr.at[m, slot], agr.at[m, slot], ag_s, ag_r.at[m], {"head": peer})
@@ -128,7 +135,24 @@
     pl.semaphore_wait(barrier, (NH - 1) + (NY - 1) + 4)
     greet(token.at[0], strides[0])
     for m in range(2):
-        each(NH, head_peer, lambda p: rs_copy(m, p, me_h).start())
+        pair_copy(m).start()
+
+    def spread_chip_sum(m):
+        drain(pair.at[m], p_r.at[m])
+        agr[m, pl.ds(me_h, 1)] = (part[m, pl.ds(core, 1)] + pair[m][None]).astype(BF16)
+        each_now(NH, head_peer, lambda p: ag_copy(m, p, me_h).start())
+
+    spread_chip_sum(0)
+
+    def projected(m):
+        drain(agr.at[m, pl.ds(0, NH - 1)], ag_r.at[m])
+        halves = []
+        for i in range(2):
+            total = agr[m, i].astype(F32)
+            for k in range(2 + i, NH, 2):
+                total = total + agr[m, k].astype(F32)
+            halves.append(total)
+        return jnp.concatenate(halves, axis=0).astype(BF16)
 
     loads[2].wait()
     loads[3].wait()
@@ -164,6 +188,7 @@
         pl.semaphore_wait(token.at[i], 2)
         greet(token.at[i + 1], stride)
 
+    spread_chip_sum(1)
     loads[4].wait()
     for q in range(HEADS // 2):
         at = pl.ds(128 * q, 128)
@@ -171,19 +196,10 @@
         scl[:, at] = s
         wgt[:, at] = (spread(tail, q) * s.astype(F32)).astype(BF16)
 
-    for m in range(2):
-        rsr[m, pl.ds(me_h, 1)] = part[m, pl.ds(me_h, 1)]
-        drain(rsr.at[m, pl.ds(0, NH - 1)], rs_r.at[m])
-        total = rsr[m, 0]
-        for k in range(1, NH):
-            total = total + rsr[m, k]
-        agr[m, pl.ds(me_h, 1)] = total.astype(BF16)[None]
-        each(NH, head_peer, lambda p: ag_copy(m, p, me_h).start())
     pl.semaphore_wait(token.at[len(strides) - 1], 2)
     each(NZ, z_peer, lambda p: d_copy(p, me_z).start())
     drecv[pl.ds(me_z, 1)] = dsend[pl.ds(lax.div(me_z, NI), 1)]
-    drain(agr.at[0, pl.ds(0, NH - 1)], ag_r.at[0])
-    b_cols = agr[0].reshape(T, STATE).astype(F32).T.astype(BF16)
+    b_cols = projected(0).astype(F32).T.astype(BF16)
 
 
     for c in range(CHUNKS):
@@ -193,8 +209,7 @@
         each(NZ, z_peer, lambda p: f_copy(c, p, me_z).start())
         frecv[c, pl.ds(me_z, 1)] = fsend[c, pl.ds(me_z, 1)]
 
-    drain(agr.at[1, pl.ds(0, NH - 1)], ag_r.at[1])
-    c_rows = agr[1].reshape(T, STATE)
+    c_rows = projected(1)
     loads[5].wait()
     scores = dot(c_rows, b_cols)
     M = T // 2
@@ -235,7 +250,7 @@
             span = drecv[k, c] * span
         ysend[c, :SR] = carry
         ysend[c, SR:] = jnp.broadcast_to(span, (8, CW))
-        each(NY, y_peer, lambda p: y_copy(c, p, me_y).start())
+        each_now(NY, y_peer, lambda p: y_copy(c, p, me_y).start())
         yrecv[c, pl.ds(me_y, 1)] = ysend[c][None]
     for c in range(CHUNKS):
         if NY > 1:
@@ -263,7 +278,7 @@
             for i in range(CW // 128):
                 squares = squares + sq[:, 128 * i:128 * i + 128]
     srecv[pl.ds(me_h, 1)] = jnp.sum(squares.T, axis=0, keepdims=True)[None]
-    each(NH, head_peer, lambda p: s_copy(p, me_h).start())
+    each_now(NH, head_peer, lambda p: s_copy(p, me_h).start())
     drain(srecv.at[pl.ds(0, NH - 1)], s_r)
     mean = srecv[0]
     for k in range(1, NH):
@@ -274,7 +289,7 @@
         at = pl.ds(128 * q, 128)
         out[:, at] = (gated_v[:, at] * scale).astype(BF16)
 
-    drain(part.at[:, pl.ds(0, NH - 1)], rs_s)
+    drain(pair, p_s)
     drain(agr.at[:, pl.ds(0, NH - 1)], ag_s)
     drain(drecv.at[pl.ds(0, NZ - 1)], d_s)
     drain(fsend.at[:, pl.ds(0, NZ - 1)], f_s)
@@ -286,7 +301,6 @@
 
 def shards(NH, NY, NZ, hidden_in, proj_weight, head_input, gate_input, step_size, decay_rate, norm_gain):
     KD = hidden_in.shape[1]
-    RB = T // NH
     SR = STATE // (NZ // 2)
     operands = (hidden_in, proj_weight, head_input, gate_input, step_size.T, decay_rate.reshape(1, HEADS), norm_gain.reshape(1, COLS))
     in_hbm = pl.BlockSpec(memory_space=pltpu.HBM)
@@ -300,7 +314,7 @@
         scratch_shapes=[
             vm((T, KD), BF16), vm((KD, 2 * STATE), BF16), vm((T, COLS), BF16), vm((T, COLS), BF16),
             vm((HEADS, T), F32), vm((1, HEADS), F32), vm((1, COLS), F32), dma((7,)),
-            vm((2, NH, RB, STATE), F32), vm((2, NH, RB, STATE), F32), vm((2, NH, RB, STATE), BF16),
+            vm((2, 2, T // 2, STATE), F32), vm((2, T // 2, STATE), F32), vm((2, NH, T // 2, STATE), BF16),
             vm((T, COLS), BF16), vm((T, COLS), BF16), vm((T, COLS), F32),
             vm((CHUNKS, NZ, SR, CW), BF16), vm((CHUNKS, NZ, SR, CW), BF16), vm((2, CHUNKS, 1, CW), F32), vm((NZ, CHUNKS, 1, CW), F32),
             vm((CHUNKS, SR + 8, CW), F32), vm((CHUNKS, NY, SR + 8, CW), F32),

time: 56 us -> 54.9 us (0.980)
  Pallas kernels: 55.1 us -> 54 us
    pallas_call x1, Pallas kernels: 55.1 us -> 54 us  [shards(): pl.pallas_call(functools.partial(kernel, NH, NY, NZ), name='layer', out_s...]
where the time goes in v5:
time: 54.9 us; the launch traced here: 54.8 us
  Pallas kernels  54 us (98%)
  local copies, waits for them, and re-layouts  0.8 us (1%)
    pallas_call x1, Pallas kernels, shards(): pl.pallas_call(functools.partial(kernel, NH, NY, NZ), name='layer', out_s...  54 us

profile of v5, /device:TPU:1, one launch (start us, length us, event | category | flops | bytes accessed | tf_op | source)
XLA Modules:
  0.0 54.8 jit_solution(2862806878717717219)
XLA Ops:
  0.0 54.0 %layer.1 = bf16[256,1024]{1,0:T(8,128)(2,1)S(1)} custom-call(bf16[256,512]{1,0:T(8,128)(2,1)} %hid.1, bf16[4096,256]{1,0:T(8,128)(2,1)} %w.1, bf16[256,1024]{1,0:T(8,128)(2,1)} %x.1, bf16[256,1024]{1,0:T(8,128)(2,1)} %g.1, f32[16,256]{1,0:T(8,128)} %bitcast.3, f32[1,16]{1,0:T(1,128)} %bitcast.5, f32[1,1024]{1,0:T(1,128)} %bitcast.4), custom_call_target="tpu_custom_call" | custom-call | tf_op jit(solution)/shard_map/layer/pallas_call | solution.py:308
  54.0 0.8 %copy.9 = bf16[256,1024]{1,0:T(8,128)(2,1)} copy(bf16[256,1024]{1,0:T(8,128)(2,1)S(1)} %layer.1) | data formatting | bytes 1048576

commit v6 on v5

--- a/solution.py
+++ b/solution.py
@@ -15,7 +15,8 @@
 HEAD_DIM = 64
 STATE = 128
 COLS = HEADS * HEAD_DIM
-CHUNKS = 2
+LAG = 1
+CHUNKS = 4
 CHUNK = COLS // CHUNKS
 CW = CHUNK // 2
 LOG2E = math.log2(math.e)
@@ -30,9 +31,9 @@
     hid, w, x, g, dt, rate, gain, out,
     hid_v, w_v, x_v, g_v, dt_v, rate_v, gain_v, in_sem,
     part, pair, agr, scl, wgt, expand,
-    fsend, frecv, dsend, drecv, ysend, yrecv, gsend, grecv,
+    fsend, frecv, dsend, drecv, zsend, zrecv, ysend, yrecv, gsend, grecv,
     acc, fac, gated_v, srecv,
-    p_s, p_r, ag_s, ag_r, d_s, d_r, f_s, f_r, y_s, y_r, g_s, g_r, s_s, s_r, token,
+    p_s, p_r, ag_s, ag_r, d_s, d_r, f_s, f_r, z_s, z_r, y_s, y_r, g_s, g_r, s_s, s_r, token,
 ):
     KD = hid_v.shape[1]
     NI = NZ // 2
@@ -47,8 +48,7 @@
         return lax.rem(me_h + r, NH)
 
     def far_first(k):
-        off = lax.div(k, 2)
-        return NZ // 2 + jnp.where(lax.rem(k, 2) == 1, off, -off)
+        return NZ // 2 + (k // 2 if k % 2 else -(k // 2))
 
     def z_peer(k):
         return lax.rem(me_z + far_first(k), NZ)
@@ -58,11 +58,6 @@
 
     def seq_id(y, z):
         return y * NZ + z
-
-    def each(n, peer_of, action):
-        @pl.loop(1, n)
-        def _(r):
-            action(peer_of(r))
 
     def each_now(n, peer_of, action):
         for r in range(1, n):
@@ -125,6 +120,9 @@
 
     def y_copy(c, peer, slot):
         return remote(ysend.at[c], yrecv.at[c, slot], y_s, y_r.at[c], {"seq": seq_id(peer, me_z)})
+
+    def span_copy(peer, slot):
+        return remote(zsend, zrecv.at[slot], z_s, z_r, {"seq": seq_id(peer, me_z)})
 
     def g_copy(c, peer, slot):
         return remote(gsend.at[c, peer], grecv.at[c, slot], g_s, g_r.at[c], {"seq": seq_id(me_y, peer)})
@@ -183,7 +181,7 @@
         at = pl.ds(128 * q, 128)
         e = spread(grow, q)
         expand[:, at] = e
-        dsend[(q % 4) // 2, q // 4, :, pl.ds(128 * (q % 2), 128)] = e[T - 1:T, :]
+        dsend[q % 2, q // 2] = e[T - 1:T, :]
     for i, stride in enumerate(strides[1:]):
         pl.semaphore_wait(token.at[i], 2)
         greet(token.at[i + 1], stride)
@@ -197,7 +195,7 @@
         wgt[:, at] = (spread(tail, q) * s.astype(F32)).astype(BF16)
 
     pl.semaphore_wait(token.at[len(strides) - 1], 2)
-    each(NZ, z_peer, lambda p: d_copy(p, me_z).start())
+    each_now(NZ, z_peer, lambda p: d_copy(p, me_z).start())
     drecv[pl.ds(me_z, 1)] = dsend[pl.ds(lax.div(me_z, NI), 1)]
     b_cols = projected(0).astype(F32).T.astype(BF16)
 
@@ -206,7 +204,7 @@
         fresh = dot(b_cols, wgt[:, pl.ds(CHUNK * c, CHUNK)]).astype(BF16)
         for j in range(2):
             fsend[c, pl.ds(NI * j, NI)] = fresh[:, CW * j:CW * j + CW].reshape(NI, SR, CW)
-        each(NZ, z_peer, lambda p: f_copy(c, p, me_z).start())
+        each_now(NZ, z_peer, lambda p: f_copy(c, p, me_z).start())
         frecv[c, pl.ds(me_z, 1)] = fsend[c, pl.ds(me_z, 1)]
 
     c_rows = projected(1)
@@ -241,29 +239,41 @@
         acc[M:, at] = lower * silu[M:]
 
     drain(drecv.at[pl.ds(0, NZ - 1)], d_r)
-    for c in range(CHUNKS):
+    span = drecv[0]
+    for k in range(1, NZ):
+        span = span * drecv[k]
+    zsend[...] = span
+    each_now(NY, y_peer, lambda p: span_copy(p, me_y).start())
+    zrecv[pl.ds(me_y, 1)] = zsend[...][None]
+    def total_of_row(c):
         drain(frecv.at[c, pl.ds(0, NZ - 1)], f_r.at[c])
         carry = frecv[c, 0].astype(F32)
-        span = drecv[0, c]
         for k in range(1, NZ):
             carry = drecv[k, c] * carry + frecv[c, k].astype(F32)
-            span = drecv[k, c] * span
-        ysend[c, :SR] = carry
-        ysend[c, SR:] = jnp.broadcast_to(span, (8, CW))
+        ysend[c] = carry
         each_now(NY, y_peer, lambda p: y_copy(c, p, me_y).start())
         yrecv[c, pl.ds(me_y, 1)] = ysend[c][None]
-    for c in range(CHUNKS):
+
+    def entering_states(c):
         if NY > 1:
             drain(yrecv.at[c, pl.ds(0, NY - 1)], y_r.at[c])
         carry = jnp.zeros((SR, CW), F32)
         for k in range(NY - 1):
-            later = yrecv[c, k, SR:SR + 1] * carry + yrecv[c, k, :SR]
+            later = zrecv[k, c] * carry + yrecv[c, k]
             carry = jnp.where(k < me_y, later, carry)
         for k in range(NZ):
             gsend[c, k] = carry.astype(BF16)
             carry = drecv[k, c] * carry + frecv[c, k].astype(F32)
-        each(NZ, z_peer, lambda p: g_copy(c, p, me_z).start())
+        each_now(NZ, z_peer, lambda p: g_copy(c, p, me_z).start())
         grecv[c, pl.ds(me_z, 1)] = gsend[c, pl.ds(me_z, 1)]
+
+    for c in range(CHUNKS + LAG):
+        if c < CHUNKS:
+            total_of_row(c)
+        if c == 0 and NY > 1:
+            drain(zrecv.at[pl.ds(0, NY - 1)], z_r)
+        if c >= LAG:
+            entering_states(c - LAG)
 
     loads[6].wait()
     squares = jnp.zeros((T, 128), F32)
@@ -297,6 +307,7 @@
     drain(srecv.at[pl.ds(0, NH - 1)], s_s)
     if NY > 1:
         drain(yrecv.at[:, pl.ds(0, NY - 1)], y_s)
+        drain(zrecv.at[pl.ds(0, NY - 1)], z_s)
 
 
 def shards(NH, NY, NZ, hidden_in, proj_weight, head_input, gate_input, step_size, decay_rate, norm_gain):
@@ -317,10 +328,10 @@
             vm((2, 2, T // 2, STATE), F32), vm((2, T // 2, STATE), F32), vm((2, NH, T // 2, STATE), BF16),
             vm((T, COLS), BF16), vm((T, COLS), BF16), vm((T, COLS), F32),
             vm((CHUNKS, NZ, SR, CW), BF16), vm((CHUNKS, NZ, SR, CW), BF16), vm((2, CHUNKS, 1, CW), F32), vm((NZ, CHUNKS, 1, CW), F32),
-            vm((CHUNKS, SR + 8, CW), F32), vm((CHUNKS, NY, SR + 8, CW), F32),
+            vm((CHUNKS, 1, CW), F32), vm((NY, CHUNKS, 1, CW), F32), vm((CHUNKS, SR, CW), F32), vm((CHUNKS, NY, SR, CW), F32),
             vm((CHUNKS, NZ, SR, CW), BF16), vm((CHUNKS, NZ, SR, CW), BF16),
             vm((T, COLS), F32), vm((T, COLS), F32), vm((T, COLS), F32), vm((NH, 1, T), F32),
-            dma, dma((2,)), dma, dma((2,)), dma, dma, dma, dma((CHUNKS,)), dma, dma((CHUNKS,)), dma, dma((CHUNKS,)), dma, dma,
+            dma, dma((2,)), dma, dma((2,)), dma, dma, dma, dma((CHUNKS,)), dma, dma, dma, dma((CHUNKS,)), dma, dma((CHUNKS,)), dma, dma,
             pltpu.SemaphoreType.REGULAR((2,)),
         ],
         compiler_params=pltpu.CompilerParams(collective_id=0, has_side_effects=True, vmem_limit_bytes=20 * 2**20),

time: 54.9 us -> 52.9 us (0.964)
  Pallas kernels: 54 us -> 51.9 us
    pallas_call x1, Pallas kernels: 54 us -> 51.9 us  [shards(): pl.pallas_call(functools.partial(kernel, NH, NY, NZ), name='layer', out_s...]
where the time goes in v6:
time: 52.9 us; the launch traced here: 52.7 us
  Pallas kernels  51.9 us (98%)
  local copies, waits for them, and re-layouts  0.8 us (2%)
    pallas_call x1, Pallas kernels, shards(): pl.pallas_call(functools.partial(kernel, NH, NY, NZ), name='layer', out_s...  51.9 us

profile of v6, /device:TPU:1, one launch (start us, length us, event | category | flops | bytes accessed | tf_op | source)
XLA Modules:
  0.0 52.7 jit_solution(11623144608997838331)
XLA Ops:
  0.0 51.9 %layer.1 = bf16[256,1024]{1,0:T(8,128)(2,1)S(1)} custom-call(bf16[256,512]{1,0:T(8,128)(2,1)} %hid.1, bf16[4096,256]{1,0:T(8,128)(2,1)} %w.1, bf16[256,1024]{1,0:T(8,128)(2,1)} %x.1, bf16[256,1024]{1,0:T(8,128)(2,1)} %g.1, f32[16,256]{1,0:T(8,128)} %bitcast.3, f32[1,16]{1,0:T(1,128)} %bitcast.5, f32[1,1024]{1,0:T(1,128)} %bitcast.4), custom_call_target="tpu_custom_call" | custom-call | tf_op jit(solution)/shard_map/layer/pallas_call | solution.py:319
  51.9 0.8 %copy.9 = bf16[256,1024]{1,0:T(8,128)(2,1)} copy(bf16[256,1024]{1,0:T(8,128)(2,1)S(1)} %layer.1) | data formatting | bytes 1048576

commit v7 on v6

--- a/solution.py
+++ b/solution.py
@@ -83,11 +83,9 @@
         for step in (distance, NZ - distance):
             signal(sem, {"seq": seq_id(me_y, lax.rem(me_z + step, NZ))})
 
-    greet(barrier, 1)
-    greet(barrier, 2)
-    strides = []
-    while 2 * 2 ** len(strides) < NZ // 2:
-        strides.append(2 * 2 ** len(strides))
+    for near in range(1, 5):
+        greet(barrier, near)
+    strides = [4]
     each_now(NY, y_peer, lambda p: signal(barrier, {"seq": seq_id(p, me_z)}))
     each_now(NH, head_peer, lambda p: signal(barrier, {"head": p}))
 
@@ -130,7 +128,7 @@
     def s_copy(peer, slot):
         return remote(srecv.at[slot], srecv.at[slot], s_s, s_r, {"head": peer})
 
-    pl.semaphore_wait(barrier, (NH - 1) + (NY - 1) + 4)
+    pl.semaphore_wait(barrier, (NH - 1) + (NY - 1) + 8)
     greet(token.at[0], strides[0])
     for m in range(2):
         pair_copy(m).start()

time: 52.9 us -> 52.6 us (level)
  no operation moved by 1% of the time
where the time goes in v7:
time: 52.6 us; the launch traced here: 52.5 us
  Pallas kernels  51.7 us (98%)
  local copies, waits for them, and re-layouts  0.8 us (2%)
    pallas_call x1, Pallas kernels, shards(): pl.pallas_call(functools.partial(kernel, NH, NY, NZ), name='layer', out_s...  51.7 us

profile of v7, /device:TPU:1, one launch (start us, length us, event | category | flops | bytes accessed | tf_op | source)
XLA Modules:
  0.0 52.5 jit_solution(7661731555777030808)
XLA Ops:
  0.0 51.7 %layer.1 = bf16[256,1024]{1,0:T(8,128)(2,1)S(1)} custom-call(bf16[256,512]{1,0:T(8,128)(2,1)} %hid.1, bf16[4096,256]{1,0:T(8,128)(2,1)} %w.1, bf16[256,1024]{1,0:T(8,128)(2,1)} %x.1, bf16[256,1024]{1,0:T(8,128)(2,1)} %g.1, f32[16,256]{1,0:T(8,128)} %bitcast.3, f32[1,16]{1,0:T(1,128)} %bitcast.5, f32[1,1024]{1,0:T(1,128)} %bitcast.4), custom_call_target="tpu_custom_call" | custom-call | tf_op jit(solution)/shard_map/layer/pallas_call | solution.py:317
  51.7 0.8 %copy.9 = bf16[256,1024]{1,0:T(8,128)(2,1)} copy(bf16[256,1024]{1,0:T(8,128)(2,1)S(1)} %layer.1) | data formatting | bytes 1048576
